TPU v7x, 512 devices: a whole 4x4x16 slice. The times are simulated.
512 devices in a mesh: layer: 32 (over y, x, core), latent: 16 (over z).
Axes of the slice: x: 4, y: 4, z: 16, core: 2. Of those that a mesh axis runs over, the one named last changes fastest.
Arguments:
- layer_input: bfloat16 [32, 1024, 4096], P('layer', None, 'latent'), may hold values from -6 to 6
- enc_weight: bfloat16 [32, 4096, 2048], P('layer', None, 'latent'), may hold values from -0.09375 to 0.09375
- enc_bias: float32 [32, 2048], P('layer', 'latent'), may hold values from -3 to 3
- dec_weight: bfloat16 [32, 3, 2048, 4096], P('layer', None, None, 'latent'), may hold values from -0.25 to 0.25
- block_lists: int32 [32, 16, 8], P('layer'), may hold values from 0 to 15, as said below
- block_counts: int32 [32, 16], P('layer'), may hold values from 1 to 8, as said below
Outputs:
- rebuilt: bfloat16 [32, 1024, 4096], P('layer', None, 'latent')
Inputs may be any that keep to these rules, and one draw needn't show every extreme that they name: `block_lists`: each list holds distinct block ids of one layer. `block_counts`: some entry equals 8 in every draw.
All inputs are finite; a program needn't handle non-finite values.
Results may differ from a plain program's by a relative error of at most 0.0055.
Values may be sent and summed in bfloat16 or wider, within the bound.
A program may use at most 128 MiB of HBM per device.

v0:
```python
import jax
import jax.numpy as jnp
from jax import lax
from jax.sharding import PartitionSpec as P


def passed_along(value, axis, steps):
    count = lax.axis_size(axis)
    initial, last = (max(0, -steps), min(count, count - steps))
    return lax.ppermute(value, axis, [(source, source + steps) for source in range(initial, last)])


def shards(layer_input, enc_weight, enc_bias, dec_weight, block_lists, block_counts):
    encoder = enc_weight[0]
    tokens = layer_input.shape[1]
    block_width = encoder.shape[1]
    weight_rows = encoder
    preact = jnp.dot(
        lax.all_gather(layer_input, "latent", axis=2, tiled=True)[0],
        weight_rows,
        preferred_element_type=jnp.float32,
    )
    preact = preact + enc_bias[0][None, :]
    own_block = lax.axis_index("latent")
    active_ids = block_lists[0]
    counts = block_counts[0]
    slot_ids = jnp.arange(active_ids.shape[1])
    in_count = slot_ids[None, :] < counts[:, None]
    matched = (active_ids == own_block) & in_count
    tile_hit = jnp.any(matched, axis=1).astype(jnp.float32)
    tile_count = active_ids.shape[0]
    latent_act = (
        (
            jnp.maximum(preact, 0.0).reshape(tile_count, tokens // tile_count, block_width)
            * tile_hit[:, None, None]
        )
        .reshape(tokens, block_width)
        .astype(jnp.bfloat16)
    )
    decoder = dec_weight[0]
    targets = decoder.shape[0]
    weight_rows = decoder
    partials = jnp.einsum(
        "tk,skd->std",
        lax.all_gather(latent_act, "latent", axis=1, tiled=True),
        weight_rows,
        preferred_element_type=jnp.float32,
    )
    rebuilt = partials[0]
    for offset in range(1, targets):
        arrived = passed_along(partials[offset].astype(jnp.bfloat16), "layer", offset)
        rebuilt = rebuilt + arrived.astype(jnp.float32)
    return rebuilt.astype(jnp.bfloat16)[None]


def solution(mesh):
    placed = (
        P("layer", None, "latent"),
        P("layer", None, "latent"),
        P("layer", "latent"),
        P("layer", None, None, "latent"),
        P("layer", None, None),
        P("layer", None),
    )
    return jax.shard_map(
        shards, mesh=mesh, in_specs=placed, out_specs=P("layer", None, "latent"), check_vma=False
    )
```

profile of v0, /device:TPU:9, one launch (start us, length us, event | category | flops | bytes accessed | tf_op | source)
XLA Modules:
  0.0 277.0 jit_solution(11785571274011899842)
XLA Ops:
  6.5 0.0 copy-start
  6.5 0.0 all-gather.3.cloned.1.call-start
  6.5 0.7 all-gather.3.cloned.1.call-update
  7.3 0.0 all-gather.5.cloned.1.call-start
  7.3 0.9 fusion.28
  8.2 0.1 mul.13
  8.3 0.1 mul.14
  8.3 123.7 %all-gather.3.cloned.1.call-done = bf16[1,1024,4096]{2,1,0:T(8,128)(2,1)} async-done(((bf16[1,1024,256]{2,1,0:T(8,128)(2,1)}), bf16[1,1024,4096]{2,1,0:T(8,128)(2,1)}) %all-gather.3.cloned.1.call-update) | async-done | bytes 8388624 | tf_op jit(solution)/shard_map/all_gather | solution.py:19
  132.1 6.8 %fusion.19 = bf16[1024,128]{1,0:T(8,128)(2,1)} fusion(bf16[1,1024,4096]{2,1,0:T(8,128)(2,1)} %all-gather.3.cloned.1.call-done, bf16[1,4096,128]{2,1,0:T(8,128)(2,1)} %param.7, f32[1024]{0:T(1024)S(1)} %mul.14, f32[128]{0:T(128)} %bitcast.51), kind=kOutput, calls=%fused_computation.9 | convolution fusion | flops 1074266112 | bytes 9703936 | tf_op jit(solution)/shard_map/dot_general | solution.py:18
  138.8 0.0 all-gather.5.cloned.1.call-update
  138.9 92.0 %all-gather.5.cloned.1.call-done = bf16[1024,2048]{1,0:T(8,128)(2,1)} async-done(((bf16[1024,128]{1,0:T(8,128)(2,1)}), bf16[1024,2048]{1,0:T(8,128)(2,1)}) %all-gather.5.cloned.1.call-update) | async-done | bytes 4194320 | tf_op jit(solution)/shard_map/all_gather | solution.py:45
  230.9 0.0 copy-done
  230.9 5.2 %fusion.29 = (bf16[3,1024,256]{2,1,0:T(8,128)(2,1)S(1)}, f32[3,1024,256]{2,1,0:T(8,128)S(1)}) fusion(bf16[1,3,2048,256]{3,2,1,0:T(8,128)(2,1)S(1)} %copy-done, bf16[1024,2048]{1,0:T(8,128)(2,1)} %all-gather.5.cloned.1.call-done), kind=kOutput, calls=%fused_computation.21 | convolution fusion | flops 3222011904 | bytes 12058624 | tf_op jit(solution)/shard_map/tk,skd->std/dot_general | solution.py:43
  236.1 0.1 slice_bitcast_fusion.2
  236.2 12.8 %collective-permute-start = (bf16[1024,256]{1,0:T(8,128)(2,1)S(1)}, bf16[1024,256]{1,0:T(8,128)(2,1)S(1)}, u32[]{:S(2)}, u32[]{:S(2)}) collective-permute-start(bf16[1024,256]{1,0:T(8,128)(2,1)S(1)} %get-tuple-element.5), channel_id=1, source_target_pairs={{0,16},{16,32},{32,48},{48,64},{64,80},{80,96},{96,112},{112,128},... | collective-permute-start | bytes 1572872 | tf_op jit(solution)/shard_map/ppermute | solution.py:10
  249.0 3.1 %collective-permute-start.1 = (bf16[1024,256]{1,0:T(8,128)(2,1)S(1)}, bf16[1024,256]{1,0:T(8,128)(2,1)S(1)}, u32[]{:S(2)}, u32[]{:S(2)}) collective-permute-start(bf16[1024,256]{1,0:T(8,128)(2,1)S(1)} %get-tuple-element.6), channel_id=1, source_target_pairs={{0,32},{16,48},{32,64},{48,80},{64,96},{80,112},{96,128},{112,144}... | collective-permute-start | bytes 1572872 | tf_op jit(solution)/shard_map/ppermute | solution.py:10
  252.1 6.1 %collective-permute-done = bf16[1024,256]{1,0:T(8,128)(2,1)S(1)} collective-permute-done((bf16[1024,256]{1,0:T(8,128)(2,1)S(1)}, bf16[1024,256]{1,0:T(8,128)(2,1)S(1)}, u32[]{:S(2)}, u32[]{:S(2)}) %collective-permute-start) | collective-permute-done | bytes 524320 | tf_op jit(solution)/shard_map/ppermute | solution.py:10
  258.2 11.0 %collective-permute-done.1 = bf16[1024,256]{1,0:T(8,128)(2,1)S(1)} collective-permute-done((bf16[1024,256]{1,0:T(8,128)(2,1)S(1)}, bf16[1024,256]{1,0:T(8,128)(2,1)S(1)}, u32[]{:S(2)}, u32[]{:S(2)}) %collective-permute-start.1) | collective-permute-done | bytes 524320 | tf_op jit(solution)/shard_map/ppermute | solution.py:10
  269.2 1.0 fusion.26
  (1 shorter events, 0.0 us)
Async XLA Ops:
  6.5 224.4 %copy-start = (bf16[1,3,2048,256]{3,2,1,0:T(8,128)(2,1)S(1)}, bf16[1,3,2048,256]{3,2,1,0:T(8,128)(2,1)}, u32[]{:S(2)}) copy-start(bf16[1,3,2048,256]{3,2,1,0:T(8,128)(2,1)} %param.9) | copy-start | bytes 9437188
  6.5 125.5 %all-gather.3.cloned.1.call-start = ((), (), s32[]{:S(2)}) async-start(), calls=%async_computation | async-start | bytes 8912896 | tf_op jit(solution)/shard_map/all_gather | solution.py:19
  7.3 223.7 %all-gather.5.cloned.1.call-start = ((), (), s32[]{:S(2)}) async-start(), calls=%async_computation.1 | async-start | bytes 4456448 | tf_op jit(solution)/shard_map/all_gather | solution.py:45
  236.2 22.0 %collective-permute-start = (bf16[1024,256]{1,0:T(8,128)(2,1)S(1)}, bf16[1024,256]{1,0:T(8,128)(2,1)S(1)}, u32[]{:S(2)}, u32[]{:S(2)}) collective-permute-start(bf16[1024,256]{1,0:T(8,128)(2,1)S(1)} %get-tuple-element.5), channel_id=1, source_target_pairs={{0,16},{16,32},{32,48},{48,64},{64,80},{80,96},{96,112},{112,128},... | collective-permute-start | bytes 1572872 | tf_op jit(solution)/shard_map/ppermute | solution.py:10
  249.0 20.2 %collective-permute-start.1 = (bf16[1024,256]{1,0:T(8,128)(2,1)S(1)}, bf16[1024,256]{1,0:T(8,128)(2,1)S(1)}, u32[]{:S(2)}, u32[]{:S(2)}) collective-permute-start(bf16[1024,256]{1,0:T(8,128)(2,1)S(1)} %get-tuple-element.6), channel_id=1, source_target_pairs={{0,32},{16,48},{32,64},{48,80},{64,96},{80,112},{96,128},{112,144}... | collective-permute-start | bytes 1572872 | tf_op jit(solution)/shard_map/ppermute | solution.py:10
Sparse Core Ops, SparseCore 0:
  9.3 122.6 all-gather.2
  139.0 91.8 all-gather.4
where the time goes:
time: 277 us
  waiting for transfers between devices  234 us (84%)
  starting transfers between devices  15.9 us (6%)
  between operations  13.4 us (5%)
  matrix products  12 us (4%)
    all_gather x1, waiting for transfers between devices, shards(): lax.all_gather(layer_input, 'latent', axis=2, tiled=True)[0]  124 us
    all_gather x1, waiting for transfers between devices, shards(): lax.all_gather(latent_act, 'latent', axis=1, tiled=True)  92 us
    ppermute x2, waiting for transfers between devices, passed_along(): lax.ppermute(value, axis, [(source, source + steps) for source in range(i...  17.1 us
    ppermute x2, starting transfers between devices, passed_along(): lax.ppermute(value, axis, [(source, source + steps) for source in range(i...  15.9 us
    dot_general x1, matrix products, shards(): jnp.dot(lax.all_gather(layer_input, 'latent', axis=2, tiled=True)[0], wei...  6.77 us
  transfers between devices with their start and end apart: 4, of which 4 were waited for; matrix products, arithmetic and copies ran while one was open for 0% of the time, Pallas kernels for 0%

commit v1 on v0

--- a/solution.py
+++ b/solution.py
@@ -42,7 +42,10 @@
     weight_rows = decoder
     partials = jnp.einsum(
         "tk,skd->std",
-        lax.all_gather(latent_act, "latent", axis=1, tiled=True),
+        jnp.concatenate(
+            lax.all_to_all(jnp.stack([latent_act] * lax.axis_size("latent")), "latent", 0, 0),
+            axis=1,
+        ),
         weight_rows,
         preferred_element_type=jnp.float32,
     )

time: 277 us -> 382 us (1.38)
  the two profiles are of different devices: /device:TPU:9 before, /device:TPU:49 now
where the time goes in v1:
time: 382 us; the launch traced here: 381 us
  blocking collectives  180 us (47%)
  waiting for transfers between devices  141 us (37%)
  starting transfers between devices  20.9 us (5%)
  between operations  13.4 us (4%)
  local copies, waits for them, and re-layouts  13 us (3%)
  matrix products  11.3 us (3%)
    all_to_all x1, blocking collectives, shards(): lax.all_to_all(jnp.stack([latent_act] * lax.axis_size('latent')), 'latent...  180 us
    all_gather x1, waiting for transfers between devices, shards(): lax.all_gather(layer_input, 'latent', axis=2, tiled=True)[0]  123 us
    ppermute x2, starting transfers between devices, passed_along(): lax.ppermute(value, axis, [(source, source + steps) for source in range(i...  20.9 us
    ppermute x2, waiting for transfers between devices, passed_along(): lax.ppermute(value, axis, [(source, source + steps) for source in range(i...  17.2 us
    reshape x2, local copies, waits for them, and re-layouts, shards(): jnp.concatenate(lax.all_to_all(jnp.stack([latent_act] * lax.axis_size('la...  12 us
  transfers between devices with their start and end apart: 3, of which 3 were waited for; matrix products, arithmetic and copies ran while one was open for 0% of the time, Pallas kernels for 0%

profile of v1, /device:TPU:49, one launch (start us, length us, event | category | flops | bytes accessed | tf_op | source)
XLA Modules:
  0.0 381.4 jit_solution(8304597818880272882)
XLA Ops:
  6.5 0.0 copy-start
  6.5 0.0 all-gather.2.cloned.1.call-start
  6.5 0.7 all-gather.2.cloned.1.call-update
  7.3 0.9 fusion.25
  8.2 0.1 mul.13
  8.3 0.1 mul.14
  8.3 123.4 %all-gather.2.cloned.1.call-done = bf16[1,1024,4096]{2,1,0:T(8,128)(2,1)} async-done(((bf16[1,1024,256]{2,1,0:T(8,128)(2,1)}), bf16[1,1024,4096]{2,1,0:T(8,128)(2,1)}) %all-gather.2.cloned.1.call-update) | async-done | bytes 8388624 | tf_op jit(solution)/shard_map/all_gather | solution.py:19
  131.7 6.1 %fusion.16 = bf16[1024,128]{1,0:T(8,128)(2,1)S(1)} fusion(bf16[1,1024,4096]{2,1,0:T(8,128)(2,1)} %all-gather.2.cloned.1.call-done, bf16[1,4096,128]{2,1,0:T(8,128)(2,1)} %param.7, f32[1024]{0:T(1024)S(1)} %mul.14, f32[128]{0:T(128)} %bitcast.47), kind=kOutput, calls=%fused_computation.8 | convolution fusion | flops 1074266112 | bytes 9703936 | tf_op jit(solution)/shard_map/dot_general | solution.py:18
  137.8 0.8 stack.2
  138.6 179.6 %all_to_all.5 = bf16[16,1024,128]{2,1,0:T(8,128)(2,1)S(1)} all-to-all(bf16[16,1024,128]{2,1,0:T(8,128)(2,1)S(1)} %stack.2), channel_id=1, replica_groups=mesh['layer'=32,'latent'=16] {'latent'}, dimensions={0} | all-to-all | bytes 8388608 | tf_op jit(solution)/shard_map/all_to_all | solution.py:46
  318.2 4.6 %copy.7 = bf16[1024,16,128]{2,1,0:T(8,128)(2,1)} copy(bf16[1024,16,128]{2,0,1:T(8,128)(2,1)S(1)} %bitcast.45) | data formatting | bytes 8388608 | tf_op jit(solution)/shard_map/reshape | solution.py:45
  322.8 7.3 %reshape.21 = bf16[1024,2048,1]{1,0,2:T(8,128)(2,1)} reshape(bf16[1024,16,128]{2,1,0:T(8,128)(2,1)} %copy.7) | data formatting | bytes 8388608 | tf_op jit(solution)/shard_map/reshape | solution.py:45
  330.1 0.0 copy-done
  330.1 5.2 %fusion.26 = (bf16[3,1024,256]{2,1,0:T(8,128)(2,1)S(1)}, f32[3,1024,256]{2,1,0:T(8,128)S(1)}) fusion(bf16[1024,2048,1]{1,0,2:T(8,128)(2,1)} %reshape.21, bf16[1,3,2048,256]{3,2,1,0:T(8,128)(2,1)S(1)} %copy-done), kind=kOutput, calls=%fused_computation.20 | convolution fusion | flops 3222011904 | bytes 12058624 | tf_op jit(solution)/shard_map/tk,skd->std/dot_general | solution.py:43
  335.3 0.1 slice_bitcast_fusion.2
  335.4 17.8 %collective-permute-start = (bf16[1024,256]{1,0:T(8,128)(2,1)S(1)}, bf16[1024,256]{1,0:T(8,128)(2,1)S(1)}, u32[]{:S(2)}, u32[]{:S(2)}) collective-permute-start(bf16[1024,256]{1,0:T(8,128)(2,1)S(1)} %get-tuple-element.5), channel_id=1, source_target_pairs={{0,16},{16,32},{32,48},{48,64},{64,80},{80,96},{96,112},{112,128},... | collective-permute-start | bytes 1572872 | tf_op jit(solution)/shard_map/ppermute | solution.py:10
  353.2 3.1 collective-permute-start.1
  356.3 6.1 %collective-permute-done = bf16[1024,256]{1,0:T(8,128)(2,1)S(1)} collective-permute-done((bf16[1024,256]{1,0:T(8,128)(2,1)S(1)}, bf16[1024,256]{1,0:T(8,128)(2,1)S(1)}, u32[]{:S(2)}, u32[]{:S(2)}) %collective-permute-start) | collective-permute-done | bytes 524320 | tf_op jit(solution)/shard_map/ppermute | solution.py:10
  362.5 11.1 %collective-permute-done.1 = bf16[1024,256]{1,0:T(8,128)(2,1)S(1)} collective-permute-done((bf16[1024,256]{1,0:T(8,128)(2,1)S(1)}, bf16[1024,256]{1,0:T(8,128)(2,1)S(1)}, u32[]{:S(2)}, u32[]{:S(2)}) %collective-permute-start.1) | collective-permute-done | bytes 524320 | tf_op jit(solution)/shard_map/ppermute | solution.py:10
  373.5 1.0 fusion.23
  (1 shorter events, 0.0 us)
Async XLA Ops:
  6.5 323.6 %copy-start = (bf16[1,3,2048,256]{3,2,1,0:T(8,128)(2,1)S(1)}, bf16[1,3,2048,256]{3,2,1,0:T(8,128)(2,1)}, u32[]{:S(2)}) copy-start(bf16[1,3,2048,256]{3,2,1,0:T(8,128)(2,1)} %param.9) | copy-start | bytes 9437188
  6.5 125.2 %all-gather.2.cloned.1.call-start = ((), (), s32[]{:S(2)}) async-start(), calls=%async_computation.1 | async-start | bytes 8912896 | tf_op jit(solution)/shard_map/all_gather | solution.py:19
  335.4 27.0 %collective-permute-start = (bf16[1024,256]{1,0:T(8,128)(2,1)S(1)}, bf16[1024,256]{1,0:T(8,128)(2,1)S(1)}, u32[]{:S(2)}, u32[]{:S(2)}) collective-permute-start(bf16[1024,256]{1,0:T(8,128)(2,1)S(1)} %get-tuple-element.5), channel_id=1, source_target_pairs={{0,16},{16,32},{32,48},{48,64},{64,80},{80,96},{96,112},{112,128},... | collective-permute-start | bytes 1572872 | tf_op jit(solution)/shard_map/ppermute | solution.py:10
  353.2 20.3 %collective-permute-start.1 = (bf16[1024,256]{1,0:T(8,128)(2,1)S(1)}, bf16[1024,256]{1,0:T(8,128)(2,1)S(1)}, u32[]{:S(2)}, u32[]{:S(2)}) collective-permute-start(bf16[1024,256]{1,0:T(8,128)(2,1)S(1)} %get-tuple-element.6), channel_id=1, source_target_pairs={{0,32},{16,48},{32,64},{48,80},{64,96},{80,112},{96,128},{112,144}... | collective-permute-start | bytes 1572872 | tf_op jit(solution)/shard_map/ppermute | solution.py:10
Sparse Core Ops, SparseCore 0:
  9.3 122.3 all-gather.1
